TPU v7x, 32 devices: a whole 2x2x4 slice. The times are simulated.
32 devices in a mesh: mol: 2 (over y), band: 8 (over z, x), grid: 2 (over core).
Axes of the slice: x: 2, y: 2, z: 4, core: 2. Of those that a mesh axis runs over, the one named last changes fastest.
Arguments:
- orbitals: bfloat16 [32, 373248], P(('mol', 'band'), 'grid'), parts along dimension 0, may hold values from -6 to 6
- group_order: int32 [32], P('mol'), parts along dimension 0, may hold values from 0 to 15, each once
- localizer: bfloat16 [2, 16, 16], P('mol'), parts along dimension 0, may hold values from -1.5 to 1.5
- bond_keep: int32 [32, 1], P('mol'), parts along dimension 0, may hold values 0 or 1
Outputs:
- localized: bfloat16 [32, 373248], P(('mol', 'band', 'grid')), parts along dimension 0
- exchange_term: bfloat16 [32, 373248], P(('mol', 'band', 'grid')), parts along dimension 0
There are 2 independent parts, one for each index of `mol`. A program takes and returns all parts, laid end to end along the dimension named above; each array names one. Nothing has to cross between parts.
Inputs may be any that keep to these rules, and one draw needn't show every extreme that they name: A permutation; localization group g holds the orbitals group_order[g * 16 + a] for a below 16. `bond_keep`: 1 keeps a pair of orbitals, 0 screens it out.
All inputs are finite; a program needn't handle non-finite values.
Results may differ from a plain program's by a relative error of at most 0.0099.
Values may be sent and summed in bfloat16 or wider, within the bound.
No kernel may reach another device: no remote copies, remote signals or barrier semaphores. Data moves between devices by JAX's collectives and lax.ppermute only.
A program may use at most 64 MiB of HBM per device.

v0:
```python
import math, functools
import numpy as np
import jax, jax.numpy as jnp
from jax import lax
from jax.experimental import pallas as pl
from jax.experimental.pallas import tpu as pltpu
from jax.sharding import PartitionSpec as P

NG = 72
HC = NG // 2 + 1
LANES = 128
KPAD = 40
XPAIRS = NG // 2
PAIR_ROWS = 2 * NG * NG // LANES
FLAT_ROWS = NG * NG * NG // LANES
FLAT_ALLOC = PAIR_ROWS * (KPAD + 1) + 7
SCREEN = 0.0625

def tables_np():
    ang = lambda r, c: 2.0 * math.pi / NG * ((np.arange(r)[:, None] * np.arange(c)[None, :]) % NG)
    ax = ang(HC, NG)
    xt = np.stack([np.cos(ax), -np.sin(ax)])
    xf = np.zeros((2, KPAD, 2, KPAD))
    xf[:, :HC, :, :XPAIRS] = xt.reshape(2, HC, XPAIRS, 2).transpose(0, 1, 3, 2)
    xf = xf.reshape(2 * KPAD, 2 * KPAD)
    c, s = np.cos(ang(NG, NG)), np.sin(ang(NG, NG))
    def pad(b):
        out = np.zeros((2, LANES, 2, LANES))
        for i in range(2):
            for j in range(2):
                out[i, :NG, j, :NG] = b[i][j]
        return out.reshape(2 * LANES, 2 * LANES)
    fz = pad([[c, -s], [s, c]])
    iz = pad([[c, s], [-s, c]])
    yf = np.block([[c, s], [-s, c]])
    yi = np.block([[c, -s], [s, c]])
    sym = 4.0 * np.sin(math.pi / NG * np.arange(NG)) ** 2
    w = np.where((np.arange(HC) == 0) | (np.arange(HC) == NG // 2), 1.0, 2.0) / float(NG ** 3)
    kern = w[:, None, None] / (SCREEN + sym[:HC, None, None] + sym[None, :, None] + sym[None, None, :])
    kern[0, 0, 0] = 0.0
    kp = np.zeros((KPAD, NG, LANES))
    kp[:HC, :, :NG] = kern
    kp = kp.reshape(KPAD // 2, 2, NG, LANES).transpose(0, 2, 1, 3).reshape(KPAD // 2 * NG, 2 * LANES)
    b = lambda a: a.astype(np.float32).astype(jnp.bfloat16)
    return b(xf), b(xf.T), b(fz), b(iz), b(yf), b(yi), kp.astype(np.float32)

def dot(a, b):
    return jnp.dot(a, b, preferred_element_type=jnp.float32)

def cat(parts, axis):
    return jnp.concatenate(parts, axis=axis)

def potential_in_flat(flat, zre, zim, s3, x2, tabs, ZCH=10):
    xf, xi, fz, iz, yf, yi, kern = tabs
    lane = lax.broadcasted_iota(jnp.int32, (KPAD, LANES), 1)

    def piece(x0, y):
        t, s = divmod(NG * (NG * x0 + y), LANES)
        a = flat[pl.ds(t, KPAD, stride=PAIR_ROWS), :]
        if s + NG > LANES:
            b = flat[pl.ds(t + 1, KPAD, stride=PAIR_ROWS), :]
            a = jnp.where(lane >= s, a, b)
        if s:
            a = pltpu.roll(a, LANES - s, 1)
        return a

    xfv = xf[...]
    for yp in range(NG // 2):
        cols = [cat([piece(0, 2 * yp + q), piece(1, 2 * yp + q)], 0) for q in range(2)]
        res = dot(xfv, cat(cols, 1).astype(jnp.bfloat16))
        for q in range(2):
            for p, z in enumerate((zre, zim)):
                z[pl.ds(2 * yp + q, KPAD, stride=NG), :] = res[p * KPAD:(p + 1) * KPAD, q * LANES:(q + 1) * LANES]

    fzv = fz[...]
    for ch in range(KPAD // ZCH):
        rows = pl.ds(ch * ZCH * NG, ZCH * NG)
        res = dot(cat([zre[rows, :], zim[rows, :]], 1).astype(jnp.bfloat16), fzv)
        for kk in range(ZCH):
            kp, kpar = divmod(ch * ZCH + kk, 2)
            for p in range(2):
                s3[pl.ds(kp * 2 * NG + p * NG, NG), kpar * LANES:(kpar + 1) * LANES] = res[kk * NG:(kk + 1) * NG, p * LANES:(p + 1) * LANES]

    yfv, yiv = yf[...], yi[...]
    for kp in range(KPAD // 2):
        w = s3[pl.ds(kp * 2 * NG, 2 * NG), :].astype(jnp.bfloat16)
        t = dot(yfv, w)
        kk = kern[pl.ds(kp * NG, NG), :]
        t = cat([t[:NG] * kk, t[NG:] * kk], 0).astype(jnp.bfloat16)
        v = dot(yiv, t)
        for kpar in range(2):
            for p, z in enumerate((zre, zim)):
                z[pl.ds((2 * kp + kpar) * NG, NG), :] = v[p * NG:(p + 1) * NG, kpar * LANES:(kpar + 1) * LANES]

    izv = iz[...]
    for ch in range(KPAD // ZCH):
        rows = pl.ds(ch * ZCH * NG, ZCH * NG)
        res = dot(cat([zre[rows, :], zim[rows, :]], 1).astype(jnp.bfloat16), izv)
        for kk in range(ZCH):
            k = ch * ZCH + kk
            for p in range(2):
                x2[pl.ds(p * KPAD + k, NG, stride=2 * KPAD), :] = res[kk * NG:(kk + 1) * NG, p * LANES:(p + 1) * LANES]

    xiv = xi[...]
    held = [None, None]
    first_part = None
    for yp in range(NG // 2):
        rhs = cat([x2[pl.ds((2 * yp + q) * 2 * KPAD, 2 * KPAD), :] for q in range(2)], 1).astype(jnp.bfloat16)
        res = dot(xiv, rhs)
        for q in range(2):
            for x0 in range(2):
                y = 2 * yp + q
                t, s = divmod(NG * (NG * x0 + y), LANES)
                v = res[x0 * KPAD:(x0 + 1) * KPAD, q * LANES:(q + 1) * LANES]
                r = pltpu.roll(v, s, 1) if s else v
                if held[x0] is None:
                    cur = r
                else:
                    cur = jnp.where(lane >= s, r, held[x0])
                if s + NG >= LANES:
                    if x0 == 1 and y == 0:
                        x2[pl.ds(0, KPAD), :] = cur
                    else:
                        flat[pl.ds(t, KPAD, stride=PAIR_ROWS), :] = cur
                    held[x0] = r
                else:
                    held[x0] = cur
    t, s = divmod(NG * NG, LANES)
    flat[pl.ds(t, KPAD, stride=PAIR_ROWS), :] = jnp.where(lane >= s, x2[pl.ds(0, KPAD), :], held[0])


def load_flat(src, dst, bands, grids):
    half = FLAT_ROWS // grids
    rows = src.shape[1]
    for g in range(grids):
        for c in range(bands):
            n = min(rows, half - c * rows)
            if n > 0:
                dst[pl.ds(g * half + c * rows, n), :] = src[c * grids + g, pl.ds(0, n), :].astype(jnp.float32)


def round_half(v):
    return v.astype(jnp.bfloat16).astype(jnp.float32)


def mix_kernel(order_row, order_col, localizer, x, out, spread):
    count = x.shape[0]
    groups, width = localizer.shape[0], localizer.shape[1]
    here = order_row[...] == lax.broadcasted_iota(jnp.int32, (count, count), 0)
    there = order_col[...] == lax.broadcasted_iota(jnp.int32, (count, count), 1)
    to_orbital = here.astype(jnp.float32).astype(jnp.bfloat16)
    from_orbital = there.astype(jnp.float32).astype(jnp.bfloat16)
    taken = [dot(localizer[g], from_orbital[g * width:(g + 1) * width]) for g in range(groups)]
    matrix = dot(to_orbital, cat(taken, 0).astype(jnp.bfloat16)).astype(jnp.bfloat16)
    rows = out.shape[1]
    for r in range(0, rows, 16):
        n = min(16, rows - r)
        y = dot(matrix, x[:, pl.ds(r * LANES, n * LANES)])
        for t in range(n):
            spread[pl.ds((r + t) * count, count), :] = y[:, t * LANES:(t + 1) * LANES]
    for o in range(count):
        out[o] = spread[pl.ds(o, rows, stride=count), :].astype(jnp.bfloat16)


def near_kernel(bands, grids, keep, own, near, xf, xi, fz, iz, yf, yi, kern,
                part, local, flat, other, zre, zim, s3, x2):
    position = lax.axis_index("band") * grids + lax.axis_index("grid")
    flag = keep[lax.rem(position + lax.rem(position + 1, 2), keep.shape[0])].astype(jnp.float32)
    load_flat(own, other.at[0], bands, grids)
    load_flat(near, other.at[1], bands, grids)
    flat[pl.ds(FLAT_ROWS, FLAT_ALLOC - FLAT_ROWS), :] = jnp.zeros((FLAT_ALLOC - FLAT_ROWS, LANES), jnp.float32)
    local[...] = other[0, pl.ds(0, FLAT_ROWS), :].astype(jnp.bfloat16)
    part[...] = jnp.zeros_like(part)

    def step(i, carry):
        flat[pl.ds(0, FLAT_ROWS), :] = round_half(other[0, pl.ds(0, FLAT_ROWS), :] * other[i, pl.ds(0, FLAT_ROWS), :])
        potential_in_flat(flat, zre, zim, s3, x2, (xf, xi, fz, iz, yf, yi, kern))
        scale = jnp.where(i == 0, 1.0, flag)
        part[...] += scale * flat[pl.ds(0, FLAT_ROWS), :] * other[i, pl.ds(0, FLAT_ROWS), :]
        return carry

    lax.fori_loop(0, 2, step, 0)


def far_kernel(bands, grids, keep, local, far, part, xf, xi, fz, iz, yf, yi, kern,
               out, flat, other, zre, zim, s3, x2):
    position = lax.axis_index("band") * grids + lax.axis_index("grid")
    flag = keep[lax.rem(position + lax.rem(position, 2), keep.shape[0])].astype(jnp.float32)
    load_flat(far, other, bands, grids)
    flat[pl.ds(FLAT_ROWS, FLAT_ALLOC - FLAT_ROWS), :] = jnp.zeros((FLAT_ALLOC - FLAT_ROWS, LANES), jnp.float32)
    flat[pl.ds(0, FLAT_ROWS), :] = round_half(local[...].astype(jnp.float32) * other[pl.ds(0, FLAT_ROWS), :])
    potential_in_flat(flat, zre, zim, s3, x2, (xf, xi, fz, iz, yf, yi, kern))
    out[...] = (part[...] + flag * flat[pl.ds(0, FLAT_ROWS), :] * other[pl.ds(0, FLAT_ROWS), :]).astype(jnp.bfloat16)


VM = pl.BlockSpec(memory_space=pltpu.VMEM)
SM = pl.BlockSpec(memory_space=pltpu.SMEM)


def work_areas():
    return [
        pltpu.VMEM(((KPAD + 1) * NG, LANES), jnp.float32),
        pltpu.VMEM(((KPAD + 1) * NG, LANES), jnp.float32),
        pltpu.VMEM((KPAD * NG, 2 * LANES), jnp.float32),
        pltpu.VMEM(((NG + 1) * 2 * KPAD, LANES), jnp.float32),
    ]


def cost(potentials):
    return pl.CostEstimate(flops=potentials * 2_000_000_000, bytes_accessed=potentials * 12_000_000, transcendentals=0)


def body(orbitals, group_order, localizer, bond_keep):
    bands, grids = lax.axis_size("band"), lax.axis_size("grid")
    count = bands * grids
    own_rows, half = orbitals.shape
    rows = -(-(half // LANES) // bands)
    rows = -(-rows // 8) * 8
    tables = tuple(jnp.asarray(t) for t in tables_np())
    keep = bond_keep.reshape(count)

    padded = jnp.pad(orbitals, ((0, 0), (0, bands * rows * LANES - half)))
    pieces = lax.all_to_all(
        padded.reshape(own_rows, bands, rows * LANES), "band", split_axis=1, concat_axis=1, tiled=True
    )
    pieces = jnp.transpose(pieces, (1, 0, 2)).reshape(count, rows * LANES)
    mixed = pl.pallas_call(
        mix_kernel,
        out_shape=jax.ShapeDtypeStruct((count, rows, LANES), jnp.bfloat16),
        in_specs=[VM] * 4,
        out_specs=VM,
        scratch_shapes=[pltpu.VMEM(((rows + 1) * count, LANES), jnp.float32)],
        name="mix",
    )(group_order.reshape(1, count), group_order.reshape(count, 1), localizer, pieces)
    own = lax.all_to_all(mixed, ("band", "grid"), split_axis=0, concat_axis=0, tiled=True)

    swap = []
    for i in range(1, count, 2):
        swap += [(i, (i + 1) % count), ((i + 1) % count, i)]
    far = lax.ppermute(own, ("band", "grid"), swap)
    near = lax.ppermute(own, "grid", [(0, 1), (1, 0)])

    flat_shape = jax.ShapeDtypeStruct((FLAT_ROWS, LANES), jnp.float32)
    half_shape = jax.ShapeDtypeStruct((FLAT_ROWS, LANES), jnp.bfloat16)
    part, local = pl.pallas_call(
        functools.partial(near_kernel, bands, grids),
        out_shape=(flat_shape, half_shape),
        in_specs=[SM] + [VM] * 9,
        out_specs=(VM, VM),
        scratch_shapes=[
            pltpu.VMEM((FLAT_ALLOC, LANES), jnp.float32),
            pltpu.VMEM((2, FLAT_ROWS + 4, LANES), jnp.float32),
        ] + work_areas(),
        cost_estimate=cost(2),
        name="near",
    )(keep, own, near, *tables)
    total = pl.pallas_call(
        functools.partial(far_kernel, bands, grids),
        out_shape=half_shape,
        in_specs=[SM] + [VM] * 10,
        out_specs=VM,
        scratch_shapes=[
            pltpu.VMEM((FLAT_ALLOC, LANES), jnp.float32),
            pltpu.VMEM((FLAT_ROWS + 4, LANES), jnp.float32),
        ] + work_areas(),
        cost_estimate=cost(1),
        name="far",
    )(keep, local, far, part, *tables)
    return local.reshape(1, -1), total.reshape(1, -1)


def solution(mesh):
    in_specs = (P(("mol", "band"), "grid"), P("mol"), P("mol", None, None), P("mol", None))
    out_specs = (P(("mol", "band", "grid"), None), P(("mol", "band", "grid"), None))
    return jax.shard_map(body, mesh=mesh, in_specs=in_specs, out_specs=out_specs, check_vma=False)
```

profile of v0, /device:TPU:1, one launch (start us, length us, event | category | flops | bytes accessed | tf_op | source)
XLA Modules:
  0.0 105.6 jit_solution(12531049803088009870)
XLA Ops:
  0.6 0.0 copy-start.2
  0.6 2.4 %pad.4 = bf16[2,188416]{1,0:T(2,128)(2,1)} pad(bf16[2,186624]{1,0:T(2,128)(2,1)} %param.11, bf16[]{:T(256)} %constant.16.clone.1), padding=0_0x0_1792 | pad | bytes 1500162 | tf_op jit(solution)/shard_map/jit(_pad)/pad | solution.py:222
  3.0 6.3 %all-to-all-start = ((bf16[2,8,23552]{2,0,1:T(2,128)(2,1)}), bf16[2,8,23552]{2,0,1:T(2,128)(2,1)S(1)}, u32[]{:S(2)}, u32[]{:S(2)}) async-start(bf16[2,8,23552]{2,0,1:T(2,128)(2,1)} %bitcast.3), calls=%async_computation | async-start | bytes 1507328 | tf_op jit(solution)/shard_map/all_to_all | solution.py:223
  9.3 0.0 copy-done.2
  9.3 0.7 copy.14.order_col
  10.0 17.7 %all-to-all-done = bf16[2,8,23552]{2,0,1:T(2,128)(2,1)S(1)} async-done(((bf16[2,8,23552]{2,0,1:T(2,128)(2,1)}), bf16[2,8,23552]{2,0,1:T(2,128)(2,1)S(1)}, u32[]{:S(2)}, u32[]{:S(2)}) %all-to-all-start) | async-done | bytes 753696 | tf_op jit(solution)/shard_map/all_to_all | solution.py:223
  27.7 1.2 %reshape.29.x = bf16[16,23552]{1,0:T(8,128)(2,1)} reshape(bf16[8,2,23552]{2,1,0:T(2,128)(2,1)S(1)} %bitcast.15) | data formatting | bytes 1507328 | tf_op jit(solution)/shard_map/reshape | solution.py:226
  28.8 2.9 %mix.1 = bf16[16,184,128]{2,1,0:T(8,128)(2,1)} custom-call(s32[1,16]{1,0:T(1,128)} %bitcast.20, s32[16,1]{1,0:T(8,128)} %copy.14.order_col, bf16[1,16,16]{2,1,0:T(8,128)(2,1)} %localizer.1, bf16[16,23552]{1,0:T(8,128)(2,1)} %reshape.29.x), custom_call_target="tpu_custom_call" | custom-call | tf_op jit(solution)/shard_map/mix/pallas_call | solution.py:227
  31.8 25.7 %all_to_all.10.own = bf16[16,184,128]{2,1,0:T(8,128)(2,1)S(1)} all-to-all(bf16[16,184,128]{2,1,0:T(8,128)(2,1)} %mix.1), channel_id=1, replica_groups=mesh['mol'=2,'band'=8,'grid'=2] {'band','grid'}, dimensions={0} | all-to-all | bytes 1507328 | tf_op jit(solution)/shard_map/all_to_all | solution.py:235
  57.4 0.0 copy-start
  57.4 0.0 collective-permute-start
  57.4 0.8 collective-permute-start.1
  58.3 1.4 %collective-permute-done.near = bf16[16,184,128]{2,1,0:T(8,128)(2,1)S(1)} collective-permute-done((bf16[16,184,128]{2,1,0:T(8,128)(2,1)S(1)}, bf16[16,184,128]{2,1,0:T(8,128)(2,1)S(1)}, u32[]{:S(2)}, u32[]{:S(2)}) %collective-permute-start) | collective-permute-done | bytes 753696 | tf_op jit(solution)/shard_map/ppermute | solution.py:241
  59.7 0.0 copy-start.4
  59.7 0.0 copy-done
  59.7 0.9 copy-done.4
  60.5 12.3 %near.1 = (f32[2916,128]{1,0:T(8,128)}, bf16[2916,128]{1,0:T(8,128)(2,1)}) custom-call(s32[16]{0:T(128)} %bitcast.22, bf16[16,184,128]{2,1,0:T(8,128)(2,1)} %copy-done, bf16[16,184,128]{2,1,0:T(8,128)(2,1)} %copy-done.4, bf16[80,80]{1,0:T(8,128)(2,1)} %constant.17.clone.xf, bf16[80,80]{1,0:T(8,128)(2,1)} %constant.18.clone.xi, ...), custom_call_target="tpu_custom_call" | custom-call | flops 4000000000 | bytes 24000000 | tf_op jit(solution)/shard_map/near/pallas_call | solution.py:245
  72.8 3.8 %collective-permute-done.1.far = bf16[16,184,128]{2,1,0:T(8,128)(2,1)S(1)} collective-permute-done((bf16[16,184,128]{2,1,0:T(8,128)(2,1)S(1)}, bf16[16,184,128]{2,1,0:T(8,128)(2,1)S(1)}, u32[]{:S(2)}, u32[]{:S(2)}) %collective-permute-start.1) | collective-permute-done | bytes 753696 | tf_op jit(solution)/shard_map/ppermute | solution.py:240
  76.6 0.0 copy-start.3
  76.6 0.9 copy-done.3
  77.5 7.8 %far.1 = bf16[2916,128]{1,0:T(8,128)(2,1)} custom-call(s32[16]{0:T(128)} %bitcast.23, bf16[2916,128]{1,0:T(8,128)(2,1)} %get-tuple-element.4.local, bf16[16,184,128]{2,1,0:T(8,128)(2,1)} %copy-done.3, f32[2916,128]{1,0:T(8,128)} %get-tuple-element.5.part, bf16[80,80]{1,0:T(8,128)(2,1)} %constant.17.clone.xf, bf16[80,80]{1,0:T(8,128)(2,1)} %constant.18.clone.xi, ...), custom_call_target="tpu_custom_call" | custom-call | flops 2000000000 | bytes 12000000 | tf_op jit(solution)/shard_map/far/pallas_call | solution.py:257
  85.2 0.0 copy-start.1
  85.2 8.0 %copy.19 = bf16[1,1,2916,128]{3,1,2,0:T(2,128)(2,1)} copy(bf16[1,1,2916,128]{3,2,1,0:T(8,128)(2,1)} %bitcast.19) | data formatting | bytes 1492992
  93.2 0.0 copy-done.1
  93.2 12.3 %copy.20 = bf16[1,1,2916,128]{3,1,2,0:T(2,128)(2,1)} copy(bf16[1,1,2916,128]{3,2,1,0:T(8,128)(2,1)S(1)} %bitcast.18) | data formatting | bytes 1492992
Async XLA Ops:
  0.6 8.7 %copy-start.2 = (s32[16]{0:T(128)S(1)}, s32[16]{0:T(128)}, u32[]{:S(2)}) copy-start(s32[16]{0:T(128)} %param.12) | copy-start | bytes 196
  3.0 24.7 %all-to-all-start = ((bf16[2,8,23552]{2,0,1:T(2,128)(2,1)}), bf16[2,8,23552]{2,0,1:T(2,128)(2,1)S(1)}, u32[]{:S(2)}, u32[]{:S(2)}) async-start(bf16[2,8,23552]{2,0,1:T(2,128)(2,1)} %bitcast.3), calls=%async_computation | async-start | bytes 1507328 | tf_op jit(solution)/shard_map/all_to_all | solution.py:223
  57.4 2.2 %copy-start = (bf16[16,184,128]{2,1,0:T(8,128)(2,1)}, bf16[16,184,128]{2,1,0:T(8,128)(2,1)S(1)}, u32[]{:S(2)}) copy-start(bf16[16,184,128]{2,1,0:T(8,128)(2,1)S(1)} %all_to_all.10.own) | copy-start | bytes 2260996
  57.4 2.2 %collective-permute-start = (bf16[16,184,128]{2,1,0:T(8,128)(2,1)S(1)}, bf16[16,184,128]{2,1,0:T(8,128)(2,1)S(1)}, u32[]{:S(2)}, u32[]{:S(2)}) collective-permute-start(bf16[16,184,128]{2,1,0:T(8,128)(2,1)S(1)} %all_to_all.10.own), channel_id=1, source_target_pairs={{0,1},{1,0},{2,3},{3,2},{4,5},{5,4},{6,7},{7,6},{8,9},{9,8},{10,11... | collective-permute-start | bytes 2261000 | tf_op jit(solution)/shard_map/ppermute | solution.py:241
  57.4 19.1 %collective-permute-start.1 = (bf16[16,184,128]{2,1,0:T(8,128)(2,1)S(1)}, bf16[16,184,128]{2,1,0:T(8,128)(2,1)S(1)}, u32[]{:S(2)}, u32[]{:S(2)}) collective-permute-start(bf16[16,184,128]{2,1,0:T(8,128)(2,1)S(1)} %all_to_all.10.own), channel_id=1, source_target_pairs={{1,2},{2,1},{3,4},{4,3},{5,6},{6,5},{7,8},{8,7},{9,10},{10,9},{11,... | collective-permute-start | bytes 2261000 | tf_op jit(solution)/shard_map/ppermute | solution.py:240
  59.7 0.9 copy-start.4
  76.6 0.9 copy-start.3
  85.2 8.0 %copy-start.1 = (bf16[2916,128]{1,0:T(8,128)(2,1)S(1)}, bf16[2916,128]{1,0:T(8,128)(2,1)}, u32[]{:S(2)}) copy-start(bf16[2916,128]{1,0:T(8,128)(2,1)} %get-tuple-element.4.local) | copy-start | bytes 2239492
where the time goes:
time: 106 us
  local copies, waits for them, and re-layouts  26.2 us (25%)
  blocking collectives  25.7 us (24%)
  Pallas kernels  23 us (22%)
  waiting for transfers between devices  22.8 us (22%)
  starting transfers between devices  7.18 us (7%)
    all_to_all x1, blocking collectives, body(): lax.all_to_all(mixed, ('band', 'grid'), split_axis=0, concat_axis=0, tile...  25.7 us
    unnamed x12, local copies, waits for them, and re-layouts  22.1 us
    all_to_all x1, waiting for transfers between devices, body(): lax.all_to_all(padded.reshape(own_rows, bands, rows * LANES), 'band', spl...  17.7 us
    pallas_call x1, Pallas kernels, body(): pl.pallas_call(functools.partial(near_kernel, bands, grids), out_shape=(f...  12.3 us
    pallas_call x1, Pallas kernels, body(): pl.pallas_call(functools.partial(far_kernel, bands, grids), out_shape=hal...  7.78 us
    all_to_all x1, starting transfers between devices, body(): lax.all_to_all(padded.reshape(own_rows, bands, rows * LANES), 'band', spl...  6.34 us
    ppermute x1, waiting for transfers between devices, body(): far = lax.ppermute(own, ('band', 'grid'), swap)  3.76 us
    pallas_call x1, Pallas kernels, body(): pl.pallas_call(mix_kernel, out_shape=jax.ShapeDtypeStruct((count, rows, L...  2.95 us
  transfers between devices with their start and end apart: 3, of which 3 were waited for; matrix products, arithmetic and copies ran while one was open for 1% of the time, Pallas kernels for 12%

commit v1 on v0

--- a/solution.py
+++ b/solution.py
@@ -143,6 +143,14 @@
     return v.astype(jnp.bfloat16).astype(jnp.float32)
 
 
+def fill_kernel(x, out, sem):
+    half = x.shape[1]
+    copy = pltpu.make_async_copy(x, out.at[:, pl.ds(0, half)], sem)
+    copy.start()
+    out[:, pl.ds(half, out.shape[1] - half)] = jnp.zeros((x.shape[0], out.shape[1] - half), jnp.bfloat16)
+    copy.wait()
+
+
 def mix_kernel(order_row, order_col, localizer, x, out, spread):
     count = x.shape[0]
     groups, width = localizer.shape[0], localizer.shape[1]
@@ -151,25 +159,37 @@
     to_orbital = here.astype(jnp.float32).astype(jnp.bfloat16)
     from_orbital = there.astype(jnp.float32).astype(jnp.bfloat16)
     taken = [dot(localizer[g], from_orbital[g * width:(g + 1) * width]) for g in range(groups)]
-    matrix = dot(to_orbital, cat(taken, 0).astype(jnp.bfloat16)).astype(jnp.bfloat16)
+    matrix = dot(to_orbital, cat(taken, 0).astype(jnp.bfloat16))
     rows = out.shape[1]
-    for r in range(0, rows, 16):
-        n = min(16, rows - r)
-        y = dot(matrix, x[:, pl.ds(r * LANES, n * LANES)])
-        for t in range(n):
-            spread[pl.ds((r + t) * count, count), :] = y[:, t * LANES:(t + 1) * LANES]
+    copies = max(1, min(8, 128 // count))
+    if copies > 1:
+        size = copies * count
+        wide = cat([cat([matrix] * copies, 1)] * copies, 0)
+        block = lambda d: lax.broadcasted_iota(jnp.int32, (size, size), d) // count
+        matrix = jnp.where(block(0) == block(1), wide, 0.0)
+    matrix = matrix.astype(jnp.bfloat16)
+    span = rows // copies
+    for r in range(0, span, 2):
+        n = min(2, span - r)
+        stacked = cat([x[:, pl.ds((j * span + r) * LANES, n * LANES)] for j in range(copies)], 0)
+        y = dot(matrix, stacked)
+        for j in range(copies):
+            for t in range(n):
+                spread[pl.ds((j * span + r + t) * count, count), :] = y[j * count:(j + 1) * count, t * LANES:(t + 1) * LANES]
     for o in range(count):
         out[o] = spread[pl.ds(o, rows, stride=count), :].astype(jnp.bfloat16)
 
 
 def near_kernel(bands, grids, keep, own, near, xf, xi, fz, iz, yf, yi, kern,
-                part, local, flat, other, zre, zim, s3, x2):
+                part, rounded, local, flat, other, zre, zim, s3, x2):
     position = lax.axis_index("band") * grids + lax.axis_index("grid")
     flag = keep[lax.rem(position + lax.rem(position + 1, 2), keep.shape[0])].astype(jnp.float32)
     load_flat(own, other.at[0], bands, grids)
     load_flat(near, other.at[1], bands, grids)
     flat[pl.ds(FLAT_ROWS, FLAT_ALLOC - FLAT_ROWS), :] = jnp.zeros((FLAT_ALLOC - FLAT_ROWS, LANES), jnp.float32)
-    local[...] = other[0, pl.ds(0, FLAT_ROWS), :].astype(jnp.bfloat16)
+    mine = other[0, pl.ds(0, FLAT_ROWS), :].astype(jnp.bfloat16)
+    rounded[...] = mine
+    local[...] = mine.reshape(local.shape)
     part[...] = jnp.zeros_like(part)
 
     def step(i, carry):
@@ -190,7 +210,8 @@
     flat[pl.ds(FLAT_ROWS, FLAT_ALLOC - FLAT_ROWS), :] = jnp.zeros((FLAT_ALLOC - FLAT_ROWS, LANES), jnp.float32)
     flat[pl.ds(0, FLAT_ROWS), :] = round_half(local[...].astype(jnp.float32) * other[pl.ds(0, FLAT_ROWS), :])
     potential_in_flat(flat, zre, zim, s3, x2, (xf, xi, fz, iz, yf, yi, kern))
-    out[...] = (part[...] + flag * flat[pl.ds(0, FLAT_ROWS), :] * other[pl.ds(0, FLAT_ROWS), :]).astype(jnp.bfloat16)
+    total = part[...] + flag * flat[pl.ds(0, FLAT_ROWS), :] * other[pl.ds(0, FLAT_ROWS), :]
+    out[...] = total.astype(jnp.bfloat16).reshape(out.shape)
 
 
 VM = pl.BlockSpec(memory_space=pltpu.VMEM)
@@ -204,6 +225,10 @@
         pltpu.VMEM((KPAD * NG, 2 * LANES), jnp.float32),
         pltpu.VMEM(((NG + 1) * 2 * KPAD, LANES), jnp.float32),
     ]
+
+
+def room(mib):
+    return pltpu.CompilerParams(vmem_limit_bytes=mib * 1024 * 1024)
 
 
 def cost(potentials):
@@ -219,7 +244,15 @@
     tables = tuple(jnp.asarray(t) for t in tables_np())
     keep = bond_keep.reshape(count)
 
-    padded = jnp.pad(orbitals, ((0, 0), (0, bands * rows * LANES - half)))
+    padded = pl.pallas_call(
+        fill_kernel,
+        out_shape=jax.ShapeDtypeStruct((own_rows, bands * rows * LANES), jnp.bfloat16),
+        in_specs=[pl.BlockSpec(memory_space=pltpu.HBM)],
+        out_specs=VM,
+        scratch_shapes=[pltpu.SemaphoreType.DMA(())],
+        compiler_params=room(8),
+        name="fill",
+    )(orbitals)
     pieces = lax.all_to_all(
         padded.reshape(own_rows, bands, rows * LANES), "band", split_axis=1, concat_axis=1, tiled=True
     )
@@ -230,6 +263,7 @@
         in_specs=[VM] * 4,
         out_specs=VM,
         scratch_shapes=[pltpu.VMEM(((rows + 1) * count, LANES), jnp.float32)],
+        compiler_params=room(16),
         name="mix",
     )(group_order.reshape(1, count), group_order.reshape(count, 1), localizer, pieces)
     own = lax.all_to_all(mixed, ("band", "grid"), split_axis=0, concat_axis=0, tiled=True)
@@ -241,22 +275,24 @@
     near = lax.ppermute(own, "grid", [(0, 1), (1, 0)])
 
     flat_shape = jax.ShapeDtypeStruct((FLAT_ROWS, LANES), jnp.float32)
+    row_shape = jax.ShapeDtypeStruct((1, FLAT_ROWS * LANES), jnp.bfloat16)
     half_shape = jax.ShapeDtypeStruct((FLAT_ROWS, LANES), jnp.bfloat16)
-    part, local = pl.pallas_call(
+    part, rounded, local = pl.pallas_call(
         functools.partial(near_kernel, bands, grids),
-        out_shape=(flat_shape, half_shape),
+        out_shape=(flat_shape, half_shape, row_shape),
         in_specs=[SM] + [VM] * 9,
-        out_specs=(VM, VM),
+        out_specs=(VM, VM, VM),
         scratch_shapes=[
             pltpu.VMEM((FLAT_ALLOC, LANES), jnp.float32),
             pltpu.VMEM((2, FLAT_ROWS + 4, LANES), jnp.float32),
         ] + work_areas(),
         cost_estimate=cost(2),
+        compiler_params=room(28),
         name="near",
     )(keep, own, near, *tables)
     total = pl.pallas_call(
         functools.partial(far_kernel, bands, grids),
-        out_shape=half_shape,
+        out_shape=row_shape,
         in_specs=[SM] + [VM] * 10,
         out_specs=VM,
         scratch_shapes=[
@@ -264,9 +300,10 @@
             pltpu.VMEM((FLAT_ROWS + 4, LANES), jnp.float32),
         ] + work_areas(),
         cost_estimate=cost(1),
+        compiler_params=room(28),
         name="far",
-    )(keep, local, far, part, *tables)
-    return local.reshape(1, -1), total.reshape(1, -1)
+    )(keep, rounded, far, part, *tables)
+    return local, total
 
 
 def solution(mesh):

time: 106 us -> 80.4 us (0.76)
  local copies, waits for them, and re-layouts: 26.2 us -> 1.54 us
  Pallas kernels: 23 us -> 19.7 us
  waiting for transfers between devices: 22.8 us -> 25.4 us
    unnamed x12 -> x22, local copies, waits for them, and re-layouts: 22.1 us -> 1.18 us
    pad x1 -> x0, local copies, waits for them, and re-layouts: 2.36 us -> none  [body(): padded = jnp.pad(orbitals, ((0, 0), (0, bands * rows * LANES - half)))]
    ppermute x1, waiting for transfers between devices: 3.76 us -> 5.7 us  [body(): far = lax.ppermute(own, ('band', 'grid'), swap)]
    pallas_call x1, Pallas kernels: 2.95 us -> 1.13 us  [body(): pl.pallas_call(mix_kernel, out_shape=jax.ShapeDtypeStruct((count, rows, L...]
    pallas_call x1, Pallas kernels: 12.3 us -> 11.1 us  [body(): pl.pallas_call(functools.partial(near_kernel, bands, grids), out_shape=(f...]
    pallas_call x1 -> x2, Pallas kernels: 7.78 us -> 7.48 us  [the longest x1 6.28 us: body(): pl.pallas_call(functools.partial(far_kernel, bands, grids), out_shape=row...]
  transfers between devices with their start and end apart: 3 -> 3, of which waited for: 3 -> 3; matrix products, arithmetic and copies ran while one was open for 1% -> 0% of each run, Pallas kernels for 12% -> 14%
where the time goes in v1:
time: 80.4 us; the launch traced here: 80.1 us
  blocking collectives  25.5 us (32%)
  waiting for transfers between devices  25.4 us (32%)
  Pallas kernels  19.7 us (25%)
  starting transfers between devices  7.19 us (9%)
  local copies, waits for them, and re-layouts  1.54 us (2%)
    all_to_all x1, blocking collectives, body(): lax.all_to_all(mixed, ('band', 'grid'), split_axis=0, concat_axis=0, tile...  25.5 us
    all_to_all x1, waiting for transfers between devices, body(): lax.all_to_all(padded.reshape(own_rows, bands, rows * LANES), 'band', spl...  18.3 us
    pallas_call x1, Pallas kernels, body(): pl.pallas_call(functools.partial(near_kernel, bands, grids), out_shape=(f...  11.1 us
    all_to_all x1, starting transfers between devices, body(): lax.all_to_all(padded.reshape(own_rows, bands, rows * LANES), 'band', spl...  6.36 us
    pallas_call x1, Pallas kernels, body(): pl.pallas_call(functools.partial(far_kernel, bands, grids), out_shape=row...  6.28 us
    ppermute x1, waiting for transfers between devices, body(): far = lax.ppermute(own, ('band', 'grid'), swap)  5.7 us
  transfers between devices with their start and end apart: 3, of which 3 were waited for; matrix products, arithmetic and copies ran while one was open for 0% of the time, Pallas kernels for 14%

profile of v1, /device:TPU:1, one launch (start us, length us, event | category | flops | bytes accessed | tf_op | source)
XLA Modules:
  0.0 80.1 jit_solution(14562884147044352765)
XLA Ops:
  0.6 0.0 copy-start
  0.6 1.1 %copy-done = bf16[2,186624]{1,0:T(2,128)(2,1)S(1)} copy-done((bf16[2,186624]{1,0:T(2,128)(2,1)S(1)}, bf16[2,186624]{1,0:T(2,128)(2,1)}, u32[]{:S(2)}) %copy-start) | copy-done | bytes 746520
  1.7 0.0 copy-start.2
  1.8 1.2 %fill.1 = bf16[2,188416]{1,0:T(2,128)(2,1)} custom-call(bf16[2,186624]{1,0:T(2,128)(2,1)S(1)} %copy-done), custom_call_target="tpu_custom_call" | custom-call | tf_op jit(solution)/shard_map/fill/pallas_call | solution.py:247
  3.0 0.0 copy-start.1
  3.0 6.4 %all-to-all-start = ((bf16[2,8,23552]{2,0,1:T(2,128)(2,1)}), bf16[2,8,23552]{2,0,1:T(2,128)(2,1)S(1)}, u32[]{:S(2)}, u32[]{:S(2)}) async-start(bf16[2,8,23552]{2,0,1:T(2,128)(2,1)} %bitcast.3), calls=%async_computation | async-start | bytes 1507328 | tf_op jit(solution)/shard_map/all_to_all | solution.py:256
  9.3 0.0 copy-done.2
  9.3 0.1 copy.14.order_col
  9.4 18.3 %all-to-all-done = bf16[2,8,23552]{2,0,1:T(2,128)(2,1)S(1)} async-done(((bf16[2,8,23552]{2,0,1:T(2,128)(2,1)}), bf16[2,8,23552]{2,0,1:T(2,128)(2,1)S(1)}, u32[]{:S(2)}, u32[]{:S(2)}) %all-to-all-start) | async-done | bytes 753696 | tf_op jit(solution)/shard_map/all_to_all | solution.py:256
  27.7 0.3 reshape.23.x
  28.0 0.0 copy-done.1
  28.0 0.0 copy-start.3
  28.0 0.0 copy-start.4
  28.0 0.0 copy-start.5
  28.0 0.0 copy-start.6
  28.0 0.0 copy-start.7
  28.0 0.0 copy-start.8
  28.0 0.0 copy-start.9
  28.0 0.0 copy-start.10
  28.1 1.1 %mix.1 = bf16[16,184,128]{2,1,0:T(8,128)(2,1)S(1)} custom-call(s32[1,16]{1,0:T(1,128)S(1)} %bitcast.6, s32[16,1]{1,0:T(8,128)S(1)} %copy.14.order_col, bf16[1,16,16]{2,1,0:T(8,128)(2,1)S(1)} %copy-done.1, bf16[16,23552]{1,0:T(8,128)(2,1)S(1)} %reshape.23.x), custom_call_target="tpu_custom_call" | custom-call | tf_op jit(solution)/shard_map/mix/pallas_call | solution.py:260
  29.2 25.5 %all_to_all.10.own = bf16[16,184,128]{2,1,0:T(8,128)(2,1)S(1)} all-to-all(bf16[16,184,128]{2,1,0:T(8,128)(2,1)S(1)} %mix.1), channel_id=1, replica_groups=mesh['mol'=2,'band'=8,'grid'=2] {'band','grid'}, dimensions={0} | all-to-all | bytes 1507328 | tf_op jit(solution)/shard_map/all_to_all | solution.py:269
  54.7 0.0 collective-permute-start
  54.7 0.8 %collective-permute-start.1 = (bf16[16,184,128]{2,1,0:T(8,128)(2,1)S(1)}, bf16[16,184,128]{2,1,0:T(8,128)(2,1)S(1)}, u32[]{:S(2)}, u32[]{:S(2)}) collective-permute-start(bf16[16,184,128]{2,1,0:T(8,128)(2,1)S(1)} %all_to_all.10.own), channel_id=1, source_target_pairs={{1,2},{2,1},{3,4},{4,3},{5,6},{6,5},{7,8},{8,7},{9,10},{10,9},{11,... | collective-permute-start | bytes 2261000 | tf_op jit(solution)/shard_map/ppermute | solution.py:274
  55.5 1.4 %collective-permute-done.near = bf16[16,184,128]{2,1,0:T(8,128)(2,1)S(1)} collective-permute-done((bf16[16,184,128]{2,1,0:T(8,128)(2,1)S(1)}, bf16[16,184,128]{2,1,0:T(8,128)(2,1)S(1)}, u32[]{:S(2)}, u32[]{:S(2)}) %collective-permute-start) | collective-permute-done | bytes 753696 | tf_op jit(solution)/shard_map/ppermute | solution.py:275
  56.9 0.0 copy-done.3
  56.9 0.0 copy-done.4
  56.9 0.0 copy-done.5
  56.9 0.0 copy-done.6
  56.9 0.0 copy-done.7
  56.9 0.0 copy-done.8
  56.9 0.0 copy-done.9
  56.9 0.0 copy-done.10
  57.0 11.1 %near.1 = (f32[2916,128]{1,0:T(8,128)S(1)}, bf16[2916,128]{1,0:T(8,128)(2,1)S(1)}, bf16[1,373248]{1,0:T(2,128)(2,1)}) custom-call(s32[16]{0:T(128)S(1)} %bitcast.7, bf16[16,184,128]{2,1,0:T(8,128)(2,1)S(1)} %all_to_all.10.own, bf16[16,184,128]{2,1,0:T(8,128)(2,1)S(1)} %collective-permute-done.near, bf16[80,80]{1,0:T(8,128)(2,1)S(1)} %copy-done.9, ...), custom_call_target="tpu_custom_call" | custom-call | flops 4000000000 | bytes 24000000 | tf_op jit(solution)/shard_map/near/pallas_call | solution.py:280
  68.1 5.7 %collective-permute-done.1.far = bf16[16,184,128]{2,1,0:T(8,128)(2,1)S(1)} collective-permute-done((bf16[16,184,128]{2,1,0:T(8,128)(2,1)S(1)}, bf16[16,184,128]{2,1,0:T(8,128)(2,1)S(1)}, u32[]{:S(2)}, u32[]{:S(2)}) %collective-permute-start.1) | collective-permute-done | bytes 753696 | tf_op jit(solution)/shard_map/ppermute | solution.py:274
  73.8 6.3 %far.1 = bf16[1,373248]{1,0:T(2,128)(2,1)} custom-call(s32[16]{0:T(128)S(1)} %bitcast.8, bf16[2916,128]{1,0:T(8,128)(2,1)S(1)} %get-tuple-element.6.local, bf16[16,184,128]{2,1,0:T(8,128)(2,1)S(1)} %collective-permute-done.1.far, f32[2916,128]{1,0:T(8,128)S(1)} %get-tuple-element.7.part, bf16[80,80]{1,0:T(8,128)(2,1)S(1)} %copy-done.9, ...), custom_call_target="tpu_custom_call" | custom-call | flops 2000000000 | bytes 12000000 | tf_op jit(solution)/shard_map/far/pallas_call | solution.py:293
Async XLA Ops:
  0.6 1.1 %copy-start = (bf16[2,186624]{1,0:T(2,128)(2,1)S(1)}, bf16[2,186624]{1,0:T(2,128)(2,1)}, u32[]{:S(2)}) copy-start(bf16[2,186624]{1,0:T(2,128)(2,1)} %x.1) | copy-start | bytes 2239492
  1.7 7.6 %copy-start.2 = (s32[16]{0:T(128)S(1)}, s32[16]{0:T(128)}, u32[]{:S(2)}) copy-start(s32[16]{0:T(128)} %param.12) | copy-start | bytes 196
  3.0 25.0 %copy-start.1 = (bf16[1,16,16]{2,1,0:T(8,128)(2,1)S(1)}, bf16[1,16,16]{2,1,0:T(8,128)(2,1)}, u32[]{:S(2)}) copy-start(bf16[1,16,16]{2,1,0:T(8,128)(2,1)} %localizer.1) | copy-start | bytes 1540
  3.0 24.7 %all-to-all-start = ((bf16[2,8,23552]{2,0,1:T(2,128)(2,1)}), bf16[2,8,23552]{2,0,1:T(2,128)(2,1)S(1)}, u32[]{:S(2)}, u32[]{:S(2)}) async-start(bf16[2,8,23552]{2,0,1:T(2,128)(2,1)} %bitcast.3), calls=%async_computation | async-start | bytes 1507328 | tf_op jit(solution)/shard_map/all_to_all | solution.py:256
  28.0 28.9 %copy-start.3 = (s32[16,1]{0,1:T(1,128)S(1)}, s32[16,1]{0,1:T(1,128)}, u32[]{:S(2)}) copy-start(s32[16,1]{0,1:T(1,128)} %param.14) | copy-start | bytes 196
  28.0 28.9 %copy-start.4 = (f32[1440,256]{1,0:T(8,128)S(1)}, f32[1440,256]{1,0:T(8,128)}, u32[]{:S(2)}) copy-start(f32[1440,256]{1,0:T(8,128)} %constant.20.clone.kern) | copy-start | bytes 4423684
  28.0 28.9 %copy-start.5 = (bf16[256,256]{1,0:T(8,128)(2,1)S(1)}, bf16[256,256]{1,0:T(8,128)(2,1)}, u32[]{:S(2)}) copy-start(bf16[256,256]{1,0:T(8,128)(2,1)} %constant.16.clone.fz) | copy-start | bytes 393220
  28.0 28.9 %copy-start.6 = (bf16[256,256]{1,0:T(8,128)(2,1)S(1)}, bf16[256,256]{1,0:T(8,128)(2,1)}, u32[]{:S(2)}) copy-start(bf16[256,256]{1,0:T(8,128)(2,1)} %constant.17.clone.iz) | copy-start | bytes 393220
  28.0 28.9 %copy-start.7 = (bf16[144,144]{1,0:T(8,128)(2,1)S(1)}, bf16[144,144]{1,0:T(8,128)(2,1)}, u32[]{:S(2)}) copy-start(bf16[144,144]{1,0:T(8,128)(2,1)} %constant.18.clone.yf) | copy-start | bytes 124420
  28.0 28.9 %copy-start.8 = (bf16[144,144]{1,0:T(8,128)(2,1)S(1)}, bf16[144,144]{1,0:T(8,128)(2,1)}, u32[]{:S(2)}) copy-start(bf16[144,144]{1,0:T(8,128)(2,1)} %constant.19.clone.yi) | copy-start | bytes 124420
  28.0 28.9 %copy-start.9 = (bf16[80,80]{1,0:T(8,128)(2,1)S(1)}, bf16[80,80]{1,0:T(8,128)(2,1)}, u32[]{:S(2)}) copy-start(bf16[80,80]{1,0:T(8,128)(2,1)} %constant.14.clone.xf) | copy-start | bytes 38404
  28.0 28.9 %copy-start.10 = (bf16[80,80]{1,0:T(8,128)(2,1)S(1)}, bf16[80,80]{1,0:T(8,128)(2,1)}, u32[]{:S(2)}) copy-start(bf16[80,80]{1,0:T(8,128)(2,1)} %constant.15.clone.xi) | copy-start | bytes 38404
  54.7 2.2 %collective-permute-start = (bf16[16,184,128]{2,1,0:T(8,128)(2,1)S(1)}, bf16[16,184,128]{2,1,0:T(8,128)(2,1)S(1)}, u32[]{:S(2)}, u32[]{:S(2)}) collective-permute-start(bf16[16,184,128]{2,1,0:T(8,128)(2,1)S(1)} %all_to_all.10.own), channel_id=1, source_target_pairs={{0,1},{1,0},{2,3},{3,2},{4,5},{5,4},{6,7},{7,6},{8,9},{9,8},{10,11... | collective-permute-start | bytes 2261000 | tf_op jit(solution)/shard_map/ppermute | solution.py:275
  54.7 19.1 %collective-permute-start.1 = (bf16[16,184,128]{2,1,0:T(8,128)(2,1)S(1)}, bf16[16,184,128]{2,1,0:T(8,128)(2,1)S(1)}, u32[]{:S(2)}, u32[]{:S(2)}) collective-permute-start(bf16[16,184,128]{2,1,0:T(8,128)(2,1)S(1)} %all_to_all.10.own), channel_id=1, source_target_pairs={{1,2},{2,1},{3,4},{4,3},{5,6},{6,5},{7,8},{8,7},{9,10},{10,9},{11,... | collective-permute-start | bytes 2261000 | tf_op jit(solution)/shard_map/ppermute | solution.py:274
